TPU v7x, 32 devices: a whole 2x2x4 slice. The times are simulated.
32 devices in a mesh: chain: 8 (over z, y), col: 4 (over x, core).
Axes of the slice: x: 2, y: 2, z: 4, core: 2. Of those that a mesh axis runs over, the one named last changes fastest.
Arguments:
- rhs: bfloat16 [4, 8, 32, 128], P(None, 'chain'), may hold values from -6 to 6
- pattern: int32 [4, 8, 24], P(None, 'chain', 'col'), may hold values from 0 to 31, as said below
- factor: bfloat16 [4, 8, 24, 128, 128], P(None, 'chain', 'col'), may hold values from -0.1875 to 0.1875
- inverse: bfloat16 [4, 8, 128, 128], P(None, 'chain'), as said below
- level_size: int32 [6], replicated, may hold values from 1 to 8, 32 in all
Outputs:
- half_solved: bfloat16 [4, 8, 32, 128], P(None, 'chain')
- solved: bfloat16 [4, 8, 32, 128], P(None, 'chain')
Inputs may be any that keep to these rules, and one draw needn't show every extreme that they name: Among the pattern entries held by one index of chain and one index of col (all 4 of its block rows), at most 3 name block rows on any one index of chain (block row mod 8); in every such group exactly 3 name block rows on one index of chain that is common to all groups of that index of col. A block row may name a block row more than once. `inverse`: each block is lower triangular with a diagonal between 0.3 and 2.
All inputs are finite; a program needn't handle non-finite values.
Results may differ from a plain program's by a relative error of at most 0.013.
Values may be sent and summed in bfloat16 or wider, within the bound.
A program may use at most 64 MiB of HBM per device.

v0:
```python
import jax
import jax.numpy as jnp
from jax import lax
from jax.sharding import PartitionSpec as P


def level_index(positions, ends):
    return jnp.sum((positions[..., None] >= ends).astype(jnp.int32), axis=-1)


def per_device(rhs, pattern, factor, inverse, level_size):
    lane_count = lax.axis_size("chain")
    chain_pos = lax.axis_index("chain")
    row_count = rhs.shape[0]
    probe_count = rhs.shape[2]
    width = rhs.shape[3]
    entries = pattern.shape[2]
    level_count = level_size.shape[0]
    total = row_count * lane_count
    ends = jnp.cumsum(level_size)
    starts = ends - level_size
    own_rows = jnp.arange(row_count, dtype=jnp.int32) * lane_count + chain_pos
    own_level = level_index(own_rows, ends)
    columns = pattern[:, 0, :]
    column_level = level_index(columns, ends)
    keep = column_level < own_level[:, None]
    blocks = factor[:, 0]
    inverse_rows = inverse[:, 0]
    right = rhs[:, 0]
    slot_ids = jnp.arange(row_count, dtype=jnp.int32)
    lane_ids = jnp.arange(lane_count, dtype=jnp.int32)

    def locate(level):
        picked = own_level == level
        own_slot = jnp.sum(jnp.where(picked, slot_ids, 0))
        return (picked, own_slot, jnp.any(picked))

    def forward_level(level, carry):
        store, half_local = carry
        picked, own_slot, is_live = locate(level)
        wanted = keep[own_slot] & is_live
        chosen = jnp.where(
            wanted[:, None, None], store[columns[own_slot]], jnp.zeros((), jnp.bfloat16)
        )
        partial_value = jnp.einsum(
            "jpb,jcb->pc", chosen, blocks[own_slot], preferred_element_type=jnp.float32
        )
        summed = lax.psum(partial_value, "col")
        rest = (right[own_slot].astype(jnp.float32) - summed).astype(jnp.bfloat16)
        segment = jnp.dot(
            rest, inverse_rows[own_slot].T, preferred_element_type=jnp.float32
        ).astype(jnp.bfloat16)
        segment = jnp.where(is_live, segment, jnp.zeros((), jnp.bfloat16))
        front = lax.all_gather(segment[None], "chain", axis=0, tiled=True)
        half_local = jnp.where(picked[:, None, None], segment[None], half_local)
        start = starts[level]
        ordered = front[(start + lane_ids) % lane_count]
        store = lax.dynamic_update_slice_in_dim(store, ordered, start, 0)
        return (store, half_local)

    store = jnp.zeros((total + lane_count, probe_count, width), jnp.bfloat16)
    half_local = jnp.zeros((row_count, probe_count, width), jnp.bfloat16)
    store, half_local = lax.fori_loop(0, level_count, forward_level, (store, half_local))
    solved_local = jnp.zeros((row_count, probe_count, width), jnp.bfloat16)
    count = row_count * entries
    capacity = max(2, (count + lane_count - 1) // lane_count)
    slots_all = lane_count * capacity
    flat_cols = columns.reshape(count)
    flat_src = jnp.broadcast_to(own_rows[:, None], (row_count, entries)).reshape(count)
    dest = flat_cols % lane_count
    onehot = (dest[:, None] == lane_ids[None, :]).astype(jnp.int32)
    before = jnp.cumsum(onehot, axis=0) - onehot
    rank = jnp.sum(before * onehot, axis=1)
    slot = dest * capacity + rank
    select = slot[None, :] == jnp.arange(slots_all, dtype=jnp.int32)[:, None]
    sent_blocks = jnp.dot(
        select.astype(jnp.bfloat16),
        blocks.reshape(count, width * width),
        preferred_element_type=jnp.float32,
    )
    sent_blocks = sent_blocks.astype(jnp.bfloat16).reshape(lane_count, capacity, width, width)
    sent_src = jnp.sum(jnp.where(select, flat_src[None, :] + 1, 0), axis=1) - 1
    sent_dst = jnp.sum(jnp.where(select, flat_cols[None, :] + 1, 0), axis=1) - 1
    sent_meta = jnp.stack([sent_src, sent_dst], axis=1).reshape(lane_count, capacity, 2)
    home_blocks, home_meta = (
        lax.all_to_all(sent_blocks, "chain", split_axis=0, concat_axis=0, tiled=True),
        lax.all_to_all(sent_meta, "chain", split_axis=0, concat_axis=0, tiled=True),
    )
    home_blocks = home_blocks.reshape(slots_all, width, width)
    home_meta = home_meta.reshape(slots_all, 2)
    source_row = home_meta[:, 0]
    target_row = home_meta[:, 1]
    valid = source_row >= 0
    source_level = level_index(source_row, ends)
    target_level = level_index(target_row, ends)
    home_keep = valid & (target_level < source_level)
    source_lane = jnp.where(valid, source_row % lane_count, 0)
    home_slot = jnp.where(valid, target_row // lane_count, -1)

    def home_level(counter, carry):
        accum, solved_now = carry
        level = level_count - 1 - counter
        picked, own_slot, is_live = locate(level)
        summed = lax.psum(accum[own_slot], "col")
        rest = (half_local[own_slot].astype(jnp.float32) - summed).astype(jnp.bfloat16)
        segment = jnp.dot(rest, inverse_rows[own_slot], preferred_element_type=jnp.float32).astype(
            jnp.bfloat16
        )
        segment = jnp.where(is_live, segment, jnp.zeros((), jnp.bfloat16))
        solved_now = jnp.where(picked[:, None, None], segment[None], solved_now)
        front = lax.all_gather(segment[None], "chain", axis=0, tiled=True)
        active = home_keep & (source_level == level)
        incoming = front[source_lane]
        terms = jnp.einsum(
            "kpc,kcb->kpb", incoming, home_blocks, preferred_element_type=jnp.float32
        )
        spread = ((home_slot[None, :] == slot_ids[:, None]) & active[None, :]).astype(jnp.float32)
        added = jnp.dot(
            spread,
            terms.reshape(slots_all, probe_count * width),
            precision=lax.Precision.HIGHEST,
            preferred_element_type=jnp.float32,
        )
        accum = accum + added.reshape(row_count, probe_count, width)
        return (accum, solved_now)

    accum = jnp.zeros((row_count, probe_count, width), jnp.float32)
    accum, solved_local = lax.fori_loop(0, level_count, home_level, (accum, solved_local))
    return (half_local[:, None], solved_local[:, None])


def solution(mesh):
    return jax.shard_map(
        per_device,
        mesh=mesh,
        in_specs=(
            P(None, "chain", None, None),
            P(None, "chain", "col"),
            P(None, "chain", "col", None, None),
            P(None, "chain", None, None),
            P(),
        ),
        out_specs=(P(None, "chain", None, None), P(None, "chain", None, None)),
        check_vma=False,
    )
```

profile of v0, /device:TPU:0, one launch (start us, length us, event | category | flops | bytes accessed | tf_op | source)
XLA Modules:
  0.0 617.3 jit_solution(10101479652952594900)
XLA Ops:
  1.1 1.3 reduce.3
  4.0 7.3 %all-to-all-start = ((s32[8,3,2]{1,2,0:T(2,128)}), s32[8,3,2]{1,2,0:T(2,128)S(1)}, u32[]{:S(2)}, u32[]{:S(2)}) async-start(s32[8,3,2]{1,2,0:T(2,128)} %copy.16), calls=%async_computation | async-start | bytes 16384 | tf_op jit(solution)/shard_map/all_to_all | solution.py:87
  11.3 0.8 reduce-window.8
  12.1 0.8 copy.14
  14.0 1.8 fusion.43
  15.9 1.0 copy.21
  17.0 0.9 all-to-all-done
  17.8 5.3 all-to-all-start.1
  23.2 314.8 %while.35 = (s32[]{:T(128)}, bf16[40,32,128]{2,1,0:T(8,128)(2,1)S(1)}, bf16[4,32,128]{2,1,0:T(8,128)(2,1)S(1)}, s32[4]{0:T(128)S(1)}, bf16[4,32,128]{2,1,0:T(8,1...) while((s32[]{:T(128)}, ...), condition=%wide.region_7.8_spmd.clone, body=%wide.region_3.7_spmd.clone.sunk | while | flops 7424167 | bytes 878571 | solution.py:63
  23.8 0.7 fusion.82
  28.3 1.1 convolution_bitcast_fusion.2
  29.5 10.4 %psum.30 = f32[32,128]{1,0:T(8,128)S(1)} all-reduce(f32[32,128]{1,0:T(8,128)S(1)} %convolution_bitcast_fusion.2), channel_id=1, replica_groups=mesh['chain'=8,'col'=4] {'col'}, use_global_device_ids=true, to_apply=%region_6.6 | all-reduce | flops 4096 | bytes 32768 | tf_op jit(solution)/shard_map/while/body/eval_jaxpr/psum | solution.py:48
  39.9 1.5 fusion.84
  41.4 31.1 %all-gather.6 = bf16[256,128]{1,0:T(8,128)(2,1)S(1)} all-gather(bf16[32,128]{1,0:T(8,128)(2,1)S(1)} %fusion.84), channel_id=2, replica_groups=mesh['chain'=8,'col'=4] {'chain'}, dimensions={0}, use_global_device_ids=true | all-gather | bytes 73728 | tf_op jit(solution)/shard_map/while/body/eval_jaxpr/all_gather | solution.py:54
  77.0 0.7 fusion.82
  81.5 1.1 convolution_bitcast_fusion.2
  82.6 10.1 %psum.30 = f32[32,128]{1,0:T(8,128)S(1)} all-reduce(f32[32,128]{1,0:T(8,128)S(1)} %convolution_bitcast_fusion.2), channel_id=1, replica_groups=mesh['chain'=8,'col'=4] {'col'}, use_global_device_ids=true, to_apply=%region_6.6 | all-reduce | flops 4096 | bytes 32768 | tf_op jit(solution)/shard_map/while/body/eval_jaxpr/psum | solution.py:48
  92.8 1.5 fusion.84
  94.2 30.6 %all-gather.6 = bf16[256,128]{1,0:T(8,128)(2,1)S(1)} all-gather(bf16[32,128]{1,0:T(8,128)(2,1)S(1)} %fusion.84), channel_id=2, replica_groups=mesh['chain'=8,'col'=4] {'chain'}, dimensions={0}, use_global_device_ids=true | all-gather | bytes 73728 | tf_op jit(solution)/shard_map/while/body/eval_jaxpr/all_gather | solution.py:54
  129.3 0.7 fusion.82
  133.8 1.1 convolution_bitcast_fusion.2
  135.0 10.1 %psum.30 = f32[32,128]{1,0:T(8,128)S(1)} all-reduce(f32[32,128]{1,0:T(8,128)S(1)} %convolution_bitcast_fusion.2), channel_id=1, replica_groups=mesh['chain'=8,'col'=4] {'col'}, use_global_device_ids=true, to_apply=%region_6.6 | all-reduce | flops 4096 | bytes 32768 | tf_op jit(solution)/shard_map/while/body/eval_jaxpr/psum | solution.py:48
  145.1 1.5 fusion.84
  146.6 30.6 %all-gather.6 = bf16[256,128]{1,0:T(8,128)(2,1)S(1)} all-gather(bf16[32,128]{1,0:T(8,128)(2,1)S(1)} %fusion.84), channel_id=2, replica_groups=mesh['chain'=8,'col'=4] {'chain'}, dimensions={0}, use_global_device_ids=true | all-gather | bytes 73728 | tf_op jit(solution)/shard_map/while/body/eval_jaxpr/all_gather | solution.py:54
  181.6 0.7 fusion.82
  186.2 1.1 convolution_bitcast_fusion.2
  187.3 10.1 %psum.30 = f32[32,128]{1,0:T(8,128)S(1)} all-reduce(f32[32,128]{1,0:T(8,128)S(1)} %convolution_bitcast_fusion.2), channel_id=1, replica_groups=mesh['chain'=8,'col'=4] {'col'}, use_global_device_ids=true, to_apply=%region_6.6 | all-reduce | flops 4096 | bytes 32768 | tf_op jit(solution)/shard_map/while/body/eval_jaxpr/psum | solution.py:48
  197.4 1.5 fusion.84
  198.9 30.6 %all-gather.6 = bf16[256,128]{1,0:T(8,128)(2,1)S(1)} all-gather(bf16[32,128]{1,0:T(8,128)(2,1)S(1)} %fusion.84), channel_id=2, replica_groups=mesh['chain'=8,'col'=4] {'chain'}, dimensions={0}, use_global_device_ids=true | all-gather | bytes 73728 | tf_op jit(solution)/shard_map/while/body/eval_jaxpr/all_gather | solution.py:54
  234.0 0.7 fusion.82
  238.5 1.1 convolution_bitcast_fusion.2
  239.6 10.1 %psum.30 = f32[32,128]{1,0:T(8,128)S(1)} all-reduce(f32[32,128]{1,0:T(8,128)S(1)} %convolution_bitcast_fusion.2), channel_id=1, replica_groups=mesh['chain'=8,'col'=4] {'col'}, use_global_device_ids=true, to_apply=%region_6.6 | all-reduce | flops 4096 | bytes 32768 | tf_op jit(solution)/shard_map/while/body/eval_jaxpr/psum | solution.py:48
  249.8 1.5 fusion.84
  251.2 30.6 %all-gather.6 = bf16[256,128]{1,0:T(8,128)(2,1)S(1)} all-gather(bf16[32,128]{1,0:T(8,128)(2,1)S(1)} %fusion.84), channel_id=2, replica_groups=mesh['chain'=8,'col'=4] {'chain'}, dimensions={0}, use_global_device_ids=true | all-gather | bytes 73728 | tf_op jit(solution)/shard_map/while/body/eval_jaxpr/all_gather | solution.py:54
  286.3 0.7 fusion.82
  290.8 1.1 convolution_bitcast_fusion.2
  291.9 10.1 %psum.30 = f32[32,128]{1,0:T(8,128)S(1)} all-reduce(f32[32,128]{1,0:T(8,128)S(1)} %convolution_bitcast_fusion.2), channel_id=1, replica_groups=mesh['chain'=8,'col'=4] {'col'}, use_global_device_ids=true, to_apply=%region_6.6 | all-reduce | flops 4096 | bytes 32768 | tf_op jit(solution)/shard_map/while/body/eval_jaxpr/psum | solution.py:48
  302.1 1.5 fusion.84
  303.6 30.6 %all-gather.6 = bf16[256,128]{1,0:T(8,128)(2,1)S(1)} all-gather(bf16[32,128]{1,0:T(8,128)(2,1)S(1)} %fusion.84), channel_id=2, replica_groups=mesh['chain'=8,'col'=4] {'chain'}, dimensions={0}, use_global_device_ids=true | all-gather | bytes 73728 | tf_op jit(solution)/shard_map/while/body/eval_jaxpr/all_gather | solution.py:54
  338.2 278.4 %while.36 = (s32[]{:T(128)}, f32[4,32,128]{2,0,1:T(4,128)S(1)}, bf16[4,32,128]{2,1,0:T(8,128)(2,1)S(1)}, s32[24]{0:T(128)S(1)}, s32[24]{0:T(128)S(1)}, /*index=5...) while((s32[]{:T(128)}, f32[4,32,128]{2,0,1:T(4,128)S(1)}, ...), condition=%wide.region_18.19_spmd.clone.clone, body=%wide.region_14.18_spmd.clone.clone.sunk | while | flops 31024460 | bytes 2709372 | solution.py:128
  338.9 0.7 fusion.93
  341.7 10.1 %psum.31 = f32[32,128]{1,0:T(8,128)S(1)} all-reduce(f32[32,128]{1,0:T(8,128)S(1)} %bitcast.150), channel_id=1, replica_groups=mesh['chain'=8,'col'=4] {'col'}, use_global_device_ids=true, to_apply=%region_17.17 | all-reduce | flops 4096 | bytes 32768 | tf_op jit(solution)/shard_map/while/body/eval_jaxpr/psum | solution.py:104
  351.8 0.8 fusion.94
  352.6 30.5 %all-gather.7 = bf16[256,128]{1,0:T(8,128)(2,1)S(1)} all-gather(bf16[32,128]{1,0:T(8,128)(2,1)S(1)} %fusion.94), channel_id=3, replica_groups=mesh['chain'=8,'col'=4] {'chain'}, dimensions={0}, use_global_device_ids=true | all-gather | bytes 73728 | tf_op jit(solution)/shard_map/while/body/eval_jaxpr/all_gather | solution.py:111
  385.3 0.7 fusion.93
  388.1 10.1 %psum.31 = f32[32,128]{1,0:T(8,128)S(1)} all-reduce(f32[32,128]{1,0:T(8,128)S(1)} %bitcast.150), channel_id=1, replica_groups=mesh['chain'=8,'col'=4] {'col'}, use_global_device_ids=true, to_apply=%region_17.17 | all-reduce | flops 4096 | bytes 32768 | tf_op jit(solution)/shard_map/while/body/eval_jaxpr/psum | solution.py:104
  398.2 0.8 fusion.94
  399.0 30.5 %all-gather.7 = bf16[256,128]{1,0:T(8,128)(2,1)S(1)} all-gather(bf16[32,128]{1,0:T(8,128)(2,1)S(1)} %fusion.94), channel_id=3, replica_groups=mesh['chain'=8,'col'=4] {'chain'}, dimensions={0}, use_global_device_ids=true | all-gather | bytes 73728 | tf_op jit(solution)/shard_map/while/body/eval_jaxpr/all_gather | solution.py:111
  431.7 0.7 fusion.93
  434.5 10.1 %psum.31 = f32[32,128]{1,0:T(8,128)S(1)} all-reduce(f32[32,128]{1,0:T(8,128)S(1)} %bitcast.150), channel_id=1, replica_groups=mesh['chain'=8,'col'=4] {'col'}, use_global_device_ids=true, to_apply=%region_17.17 | all-reduce | flops 4096 | bytes 32768 | tf_op jit(solution)/shard_map/while/body/eval_jaxpr/psum | solution.py:104
  444.6 0.8 fusion.94
  445.4 30.5 %all-gather.7 = bf16[256,128]{1,0:T(8,128)(2,1)S(1)} all-gather(bf16[32,128]{1,0:T(8,128)(2,1)S(1)} %fusion.94), channel_id=3, replica_groups=mesh['chain'=8,'col'=4] {'chain'}, dimensions={0}, use_global_device_ids=true | all-gather | bytes 73728 | tf_op jit(solution)/shard_map/while/body/eval_jaxpr/all_gather | solution.py:111
  478.1 0.7 fusion.93
  480.9 10.1 %psum.31 = f32[32,128]{1,0:T(8,128)S(1)} all-reduce(f32[32,128]{1,0:T(8,128)S(1)} %bitcast.150), channel_id=1, replica_groups=mesh['chain'=8,'col'=4] {'col'}, use_global_device_ids=true, to_apply=%region_17.17 | all-reduce | flops 4096 | bytes 32768 | tf_op jit(solution)/shard_map/while/body/eval_jaxpr/psum | solution.py:104
  491.0 0.8 fusion.94
  491.8 30.5 %all-gather.7 = bf16[256,128]{1,0:T(8,128)(2,1)S(1)} all-gather(bf16[32,128]{1,0:T(8,128)(2,1)S(1)} %fusion.94), channel_id=3, replica_groups=mesh['chain'=8,'col'=4] {'chain'}, dimensions={0}, use_global_device_ids=true | all-gather | bytes 73728 | tf_op jit(solution)/shard_map/while/body/eval_jaxpr/all_gather | solution.py:111
  524.5 0.7 fusion.93
  527.3 10.1 %psum.31 = f32[32,128]{1,0:T(8,128)S(1)} all-reduce(f32[32,128]{1,0:T(8,128)S(1)} %bitcast.150), channel_id=1, replica_groups=mesh['chain'=8,'col'=4] {'col'}, use_global_device_ids=true, to_apply=%region_17.17 | all-reduce | flops 4096 | bytes 32768 | tf_op jit(solution)/shard_map/while/body/eval_jaxpr/psum | solution.py:104
  537.4 0.8 fusion.94
  538.2 30.5 %all-gather.7 = bf16[256,128]{1,0:T(8,128)(2,1)S(1)} all-gather(bf16[32,128]{1,0:T(8,128)(2,1)S(1)} %fusion.94), channel_id=3, replica_groups=mesh['chain'=8,'col'=4] {'chain'}, dimensions={0}, use_global_device_ids=true | all-gather | bytes 73728 | tf_op jit(solution)/shard_map/while/body/eval_jaxpr/all_gather | solution.py:111
  570.9 0.7 fusion.93
  573.7 10.1 %psum.31 = f32[32,128]{1,0:T(8,128)S(1)} all-reduce(f32[32,128]{1,0:T(8,128)S(1)} %bitcast.150), channel_id=1, replica_groups=mesh['chain'=8,'col'=4] {'col'}, use_global_device_ids=true, to_apply=%region_17.17 | all-reduce | flops 4096 | bytes 32768 | tf_op jit(solution)/shard_map/while/body/eval_jaxpr/psum | solution.py:104
  583.8 0.8 fusion.94
  584.6 30.5 %all-gather.7 = bf16[256,128]{1,0:T(8,128)(2,1)S(1)} all-gather(bf16[32,128]{1,0:T(8,128)(2,1)S(1)} %fusion.94), channel_id=3, replica_groups=mesh['chain'=8,'col'=4] {'chain'}, dimensions={0}, use_global_device_ids=true | all-gather | bytes 73728 | tf_op jit(solution)/shard_map/while/body/eval_jaxpr/all_gather | solution.py:111
  (165 shorter events, 43.7 us)
Async XLA Ops:
  4.0 13.8 %all-to-all-start = ((s32[8,3,2]{1,2,0:T(2,128)}), s32[8,3,2]{1,2,0:T(2,128)S(1)}, u32[]{:S(2)}, u32[]{:S(2)}) async-start(s32[8,3,2]{1,2,0:T(2,128)} %copy.16), calls=%async_computation | async-start | bytes 16384 | tf_op jit(solution)/shard_map/all_to_all | solution.py:87
  17.8 5.3 copy-start.2
  17.8 320.4 %all-to-all-start.1 = ((bf16[8,3,128,128]{3,2,1,0:T(8,128)(2,1)}), bf16[8,3,128,128]{3,2,1,0:T(8,128)(2,1)S(1)}, u32[]{:S(2)}, u32[]{:S(2)}) async-start(bf16[8,3,128,128]{3,2,1,0:T(8,128)(2,1)} %bitcast.42), calls=%async_computation.1 | async-start | bytes 1572864 | tf_op jit(solution)/shard_map/all_to_all | solution.py:86
  616.6 0.6 copy-start
  616.6 0.6 copy-start.1
where the time goes:
time: 619 us; the launch traced here: 617 us
  blocking collectives  489 us (79%)
  loops' own time  36 us (6%)
  other arithmetic  33.2 us (5%)
  matrix products  26.7 us (4%)
  local copies, waits for them, and re-layouts  18.2 us (3%)
  starting transfers between devices  12.6 us (2%)
    all_gather x6, blocking collectives, forward_level(): front = lax.all_gather(segment[None], 'chain', axis=0, tiled=True)  184 us
    all_gather x6, blocking collectives, home_level(): front = lax.all_gather(segment[None], 'chain', axis=0, tiled=True)  183 us
    psum x6, blocking collectives, forward_level(): summed = lax.psum(partial_value, 'col')  61.1 us
    psum x6, blocking collectives, home_level(): summed = lax.psum(accum[own_slot], 'col')  60.7 us
    another operation x1, loops' own time, per_device(): lax.fori_loop(0, level_count, forward_level, (store, half_local))  23.3 us
    another operation x1, loops' own time, per_device(): lax.fori_loop(0, level_count, home_level, (accum, solved_local))  12.7 us
  transfers between devices with their start and end apart: 2, of which 1 were waited for; matrix products, arithmetic and copies ran while one was open for 8% of the time, Pallas kernels for 0%

commit v1 on v0

v1 whole, which is shorter than its diff:
```python
import functools

import jax
import jax.numpy as jnp
from jax import lax
from jax.experimental import pallas as pl
from jax.experimental.pallas import tpu as pltpu
from jax.sharding import PartitionSpec as P

MESH = pl.DeviceIdType.MESH
F32 = jnp.float32
BF16 = jnp.bfloat16


def kernel(
    n_chain,
    n_col,
    levels,
    rhs_ref,
    pat_ref,
    fac_ref,
    inv_ref,
    size_ref,
    half_out,
    solved_out,
    fb,
    pat_v,
    pat_s,
    code_s,
    rhs_f,
    store,
    seg_send,
    seg_recv,
    acc,
    acc_recv,
    half_lv,
    sol_lv,
    half_tx,
    sol_tx,
    half_rx,
    sol_rx,
    pat_sem,
    pat_ssem,
    pat_lsem,
    loc_sem,
    fx_send,
    fx_recv,
    fo_send,
    fo_recv,
    ff_send,
    ff_recv,
    sg_send,
    sg_recv,
    ac_send,
    ac_recv,
    ho_send,
    ho_recv,
    so_send,
    so_recv,
):
    rows = rhs_ref.shape[0]
    probes = rhs_ref.shape[2]
    width = rhs_ref.shape[3]
    part = probes // n_col
    entries = fac_ref.shape[2]
    total = entries * n_col
    me = lax.axis_index("chain")
    k = lax.axis_index("col")
    far = lax.rem(k + n_col // 2, n_col)
    near = k + 1 - 2 * lax.rem(k, 2)
    near_far = lax.rem(near + n_col // 2, n_col)

    def lane(d):
        return lax.rem(me + d, n_chain)

    def column(d):
        return lax.rem(k + d, n_col)

    barrier = pltpu.get_barrier_semaphore()
    for d in range(1, n_chain):
        pl.semaphore_signal(barrier, inc=1, device_id={"chain": lane(d)}, device_id_type=MESH)
    for d in range(1, n_col):
        pl.semaphore_signal(barrier, inc=1, device_id={"col": column(d)}, device_id_type=MESH)
    pl.semaphore_wait(barrier, n_chain + n_col - 2)

    pat_copies = []
    for d in range(1, n_col):
        pat_copies.append(
            pltpu.make_async_remote_copy(
                src_ref=pat_ref,
                dst_ref=pat_v.at[d],
                send_sem=pat_ssem.at[d],
                recv_sem=pat_sem.at[d],
                device_id={"col": column(d)},
                device_id_type=MESH,
            )
        )
    for copy in pat_copies:
        copy.start()
    pat_local = [pltpu.make_async_copy(pat_ref, pat_s.at[0], pat_lsem.at[0])]
    pat_local[0].start()

    def held(row, who):
        return fb.at[row, pl.ds(who * entries, entries)]

    far_copies = []
    near_copies = []
    forwards = []
    locals_ = []
    for row in range(rows):
        far_copies.append(
            pltpu.make_async_remote_copy(
                src_ref=fac_ref.at[row, 0],
                dst_ref=held(row, k),
                send_sem=fx_send.at[row],
                recv_sem=fx_recv.at[row],
                device_id={"col": far},
                device_id_type=MESH,
            )
        )
        near_copies.append(
            pltpu.make_async_remote_copy(
                src_ref=fac_ref.at[row, 0],
                dst_ref=held(row, k),
                send_sem=fo_send.at[row],
                recv_sem=fo_recv.at[row],
                device_id={"col": near},
                device_id_type=MESH,
            )
        )
        forwards.append(
            pltpu.make_async_remote_copy(
                src_ref=held(row, far),
                dst_ref=held(row, far),
                send_sem=ff_send.at[row],
                recv_sem=ff_recv.at[row],
                device_id={"col": near},
                device_id_type=MESH,
            )
        )
        locals_.append(
            pltpu.make_async_copy(fac_ref.at[row, 0], held(row, k), loc_sem.at[row])
        )
    for copy in far_copies:
        copy.start()

    ends = []
    running = jnp.int32(0)
    for level in range(levels):
        running = running + size_ref[level]
        ends.append(running)

    def level_of(position):
        found = jnp.int32(0)
        for end in ends[:-1]:
            found = found + (position >= end).astype(jnp.int32)
        return found

    own_level = [level_of(row * n_chain + me) for row in range(rows)]
    slot = []
    live = []
    for level in range(levels):
        here = jnp.int32(0)
        count = jnp.int32(0)
        for row in range(rows):
            match = own_level[row] == level
            here = jnp.where(match, row, here)
            count = count + match.astype(jnp.int32)
        slot.append(here)
        live.append(count > 0)

    for row in range(rows):
        rhs_f[row] = rhs_ref[row, 0].astype(F32)

    def finish_forward(level, sums):
        right = rhs_f[slot[level], pl.ds(k * part, part), :]
        rest = (right - sums if sums is not None else right).astype(BF16)
        segment = lax.dot_general(
            rest, inv_ref[slot[level], 0], (((1,), (1,)), ((), ())), preferred_element_type=F32
        ).astype(BF16)
        copies = []
        if level < levels - 1:
            seg_send[level] = segment
            for d in range(1, n_chain):
                copies.append(
                    pltpu.make_async_remote_copy(
                        src_ref=seg_send.at[level],
                        dst_ref=seg_recv.at[level, d],
                        send_sem=sg_send.at[level, d],
                        recv_sem=sg_recv.at[level, d],
                        device_id={"chain": lane(d)},
                        device_id_type=MESH,
                    )
                )
            for copy in copies:
                copy.start()
        wide = segment.astype(F32)
        half_lv[level] = wide
        if level < levels - 1:
            store[level * n_chain + me] = wide
        return copies

    pending = []
    copies = finish_forward(0, None)
    for copy in near_copies:
        copy.start()
    for copy in locals_:
        copy.start()
    own = copies
    store[pl.ds(n_chain, (levels - 1) * n_chain)] = jnp.zeros(
        ((levels - 1) * n_chain, part, width), F32
    )
    acc[...] = jnp.zeros_like(acc)

    for d in range(1, n_col):
        pat_copies[d - 1].wait_recv()
        copy = pltpu.make_async_copy(pat_v.at[d], pat_s.at[d], pat_lsem.at[d])
        copy.start()
        pat_local.append(copy)
    for copy in pat_local:
        copy.wait()

    for level in range(1, levels):
        def fill(place, carry, level=level):
            who = lax.div(place, entries)
            item = lax.rem(place, entries)
            d = lax.rem(k - who + n_col, n_col)
            target = pat_s[d, slot[level], 0, item]
            code_s[level, place] = level_of(target) * n_chain + lax.rem(target, n_chain)
            return carry
        for place in range(total):
            fill(jnp.int32(place), 0)

    ready = [False] * rows

    def make_ready(upto):
        todo = [row for row in range(upto + 1) if not ready[row]]
        for row in todo:
            far_copies[row].wait_recv()
            forwards[row].start()
        for row in todo:
            locals_[row].wait()
            near_copies[row].wait_recv()
            forwards[row].wait_recv()
            ready[row] = True

    def times_rows(pieces, row):
        sums = None
        for j in range(0, total, 2):
            left = jnp.concatenate([pieces[j], pieces[j + 1]], axis=1)
            right = jnp.concatenate([fb[row, j], fb[row, j + 1]], axis=1)
            term = lax.dot_general(
                left, right, (((1,), (1,)), ((), ())), preferred_element_type=F32
            )
            sums = term if sums is None else sums + term
        return sums

    for level in range(1, levels):
        make_ready(min(level, rows - 1))
        for d in range(1, n_chain):
            own[d - 1].wait_recv()
            store[(level - 1) * n_chain + lane(n_chain - d)] = seg_recv[level - 1, d].astype(F32)
        pending += own
        pieces = [store[code_s[level, j]].astype(BF16) for j in range(total)]
        if level >= rows - 1:
            sums = times_rows(pieces, slot[level])
        else:
            sums = jnp.zeros((part, width), F32)
            for row in range(level + 1):
                sums = sums + jnp.where(slot[level] == row, times_rows(pieces, row), 0.0)
        own = finish_forward(level, sums)

    def share(tx, rx, by_level, send, recv):
        for row in range(rows):
            tx[row] = by_level[own_level[row]].astype(BF16)
        copies = [
            pltpu.make_async_remote_copy(
                src_ref=tx,
                dst_ref=rx.at[d],
                send_sem=send.at[d],
                recv_sem=recv.at[d],
                device_id={"col": column(d)},
                device_id_type=MESH,
            )
            for d in range(1, n_col)
        ]
        for copy in copies:
            copy.start()
        return copies

    group = lax.broadcasted_iota(jnp.int32, (n_chain * part, width), 0) // part
    half_copies = []
    own = []
    for level in reversed(range(levels)):
        rest = half_lv[level]
        if level < levels - 1:
            rest = rest - acc[level, pl.ds(me * part, part)]
            for d in range(1, n_chain):
                own[d - 1].wait_recv()
                rest = rest - acc_recv[level, d]
            pending += own
        solved = jnp.dot(
            rest.astype(BF16), inv_ref[slot[level], 0], preferred_element_type=F32
        ).astype(BF16).astype(F32)
        sol_lv[level] = solved
        if level == 0:
            break
        solved = jnp.where(live[level], solved, 0.0)
        tiled = jnp.concatenate([solved] * n_chain, axis=0)

        def spread(target, tiled=tiled, level=level):
            sums = acc[target]
            for j in range(0, total, 2):
                left = jnp.concatenate(
                    [
                        jnp.where(group == code_s[level, jj] - target * n_chain, tiled, 0.0).astype(BF16)
                        for jj in (j, j + 1)
                    ],
                    axis=1,
                )
                right = fb[slot[level], pl.ds(j, 2)].reshape(2 * width, width)
                sums = sums + jnp.dot(left, right, preferred_element_type=F32)
            acc[target] = sums

        spread(level - 1)
        own = [
            pltpu.make_async_remote_copy(
                src_ref=acc.at[level - 1, pl.ds(lane(d) * part, part)],
                dst_ref=acc_recv.at[level - 1, d],
                send_sem=ac_send.at[level - 1, d],
                recv_sem=ac_recv.at[level - 1, d],
                device_id={"chain": lane(d)},
                device_id_type=MESH,
            )
            for d in range(1, n_chain)
        ]
        for copy in own:
            copy.start()
        if level == levels - 1:
            half_copies = share(half_tx, half_rx, half_lv, ho_send, ho_recv)
        for target in range(level - 1):
            spread(target)

    sol_copies = share(sol_tx, sol_rx, sol_lv, so_send, so_recv)

    def collect(tx, rx, copies, out, wide):
        for row in range(rows):
            wide[row, pl.ds(k * part, part)] = tx[row].astype(F32)
        for d in range(1, n_col):
            copies[d - 1].wait_recv()
            for row in range(rows):
                wide[row, pl.ds(column(n_col - d) * part, part)] = rx[d, row].astype(F32)
        for row in range(rows):
            out[row, 0] = wide[row].astype(BF16)

    collect(half_tx, half_rx, half_copies, half_out, rhs_f)
    collect(sol_tx, sol_rx, sol_copies, solved_out, rhs_f)
    for copy in pending + pat_copies + far_copies + near_copies + forwards + half_copies + sol_copies:
        copy.wait_send()


def per_device(n_chain, n_col, rhs, pattern, factor, inverse, level_size):
    rows, _, probes, width = rhs.shape
    entries = factor.shape[2]
    levels = level_size.shape[0]
    part = probes // n_col
    total = entries * n_col
    dma = pltpu.SemaphoreType.DMA
    vmem = pl.BlockSpec(memory_space=pltpu.VMEM)
    out = jax.ShapeDtypeStruct(rhs.shape, rhs.dtype)
    return pl.pallas_call(
        functools.partial(kernel, n_chain, n_col, levels),
        out_shape=(out, out),
        in_specs=[
            vmem,
            vmem,
            pl.BlockSpec(memory_space=pl.ANY),
            vmem,
            pl.BlockSpec(memory_space=pltpu.SMEM),
        ],
        out_specs=(vmem, vmem),
        scratch_shapes=[
            pltpu.VMEM((rows, total, width, width), BF16),
            pltpu.VMEM((n_col, rows, 1, entries), jnp.int32),
            pltpu.SMEM((n_col, rows, 1, entries), jnp.int32),
            pltpu.SMEM((levels, total), jnp.int32),
            pltpu.VMEM((rows, probes, width), F32),
            pltpu.VMEM((levels * n_chain, part, width), F32),
            pltpu.VMEM((levels, part, width), BF16),
            pltpu.VMEM((levels, n_chain, part, width), BF16),
            pltpu.VMEM((levels, n_chain * part, width), F32),
            pltpu.VMEM((levels, n_chain, part, width), F32),
            pltpu.VMEM((levels, part, width), F32),
            pltpu.VMEM((levels, part, width), F32),
            pltpu.VMEM((rows, part, width), BF16),
            pltpu.VMEM((rows, part, width), BF16),
            pltpu.VMEM((n_col, rows, part, width), BF16),
            pltpu.VMEM((n_col, rows, part, width), BF16),
            dma((n_col,)),
            dma((n_col,)),
            dma((n_col,)),
            dma((rows,)),
            dma((rows,)),
            dma((rows,)),
            dma((rows,)),
            dma((rows,)),
            dma((rows,)),
            dma((rows,)),
            dma((levels, n_chain)),
            dma((levels, n_chain)),
            dma((levels, n_chain)),
            dma((levels, n_chain)),
            dma((n_col,)),
            dma((n_col,)),
            dma((n_col,)),
            dma((n_col,)),
        ],
        compiler_params=pltpu.CompilerParams(collective_id=0, has_side_effects=True),
    )(rhs, pattern, factor, inverse, level_size)


def solution(mesh):
    return jax.shard_map(
        functools.partial(per_device, mesh.shape["chain"], mesh.shape["col"]),
        mesh=mesh,
        in_specs=(
            P(None, "chain", None, None),
            P(None, "chain", "col"),
            P(None, "chain", "col", None, None),
            P(None, "chain", None, None),
            P(),
        ),
        out_specs=(P(None, "chain", None, None), P(None, "chain", None, None)),
        check_vma=False,
    )
```

time: 619 us -> 68.1 us (0.11)
  blocking collectives: 489 us -> 0 us
  Pallas kernels: 0 us -> 65.2 us
  loops' own time: 36 us -> 0 us
  other arithmetic: 33.2 us -> 0 us
  matrix products: 26.7 us -> 0 us
  local copies, waits for them, and re-layouts: 18.2 us -> 2 us
  starting transfers between devices: 12.6 us -> 0 us
    all_gather x12 -> x0, blocking collectives: 367 us -> none  [the longest x6 184 us: forward_level(): front = lax.all_gather(segment[None], 'chain', axis=0, tiled=True)]
    psum x12 -> x0, blocking collectives: 122 us -> none  [the longest x6 61.1 us: forward_level(): summed = lax.psum(partial_value, 'col')]
    pallas_call x0 -> x1, Pallas kernels: none -> 65.2 us  [per_device(): pl.pallas_call(functools.partial(kernel, n_chain, n_col, levels), out_sha...]
    another operation x2 -> x0, loops' own time: 36 us -> none  [the longest x1 23.3 us: per_device(): lax.fori_loop(0, level_count, forward_level, (store, half_local))]
    dot_general x31 -> x0, matrix products: 26.7 us -> none  [the longest x6 8.82 us: forward_level(): jnp.dot(rest, inverse_rows[own_slot].T, preferred_element_type=jnp.float32)]
    all_to_all x2 -> x0, starting transfers between devices: 12.6 us -> none  [the longest x1 7.31 us: per_device(): lax.all_to_all(sent_meta, 'chain', split_axis=0, concat_axis=0, tiled=True)]
    gather x18 -> x0, local copies, waits for them, and re-layouts: 10.2 us -> none  [the longest x6 3.51 us: home_level(): incoming = front[source_lane]]
    reduce_sum x17 -> x0, other arithmetic: 9.25 us -> none  [the longest x12 8.44 us: locate(): own_slot = jnp.sum(jnp.where(picked, slot_ids, 0))]
  transfers between devices with their start and end apart: 2 -> 0, of which waited for: 1 -> 0; matrix products, arithmetic and copies ran while one was open for 8% -> 0% of each run, Pallas kernels for 0% -> 0%
where the time goes in v1:
time: 68.1 us; the launch traced here: 67.9 us
  Pallas kernels  65.2 us (96%)
  local copies, waits for them, and re-layouts  2 us (3%)
    pallas_call x1, Pallas kernels, per_device(): pl.pallas_call(functools.partial(kernel, n_chain, n_col, levels), out_sha...  65.2 us
    unnamed x4, local copies, waits for them, and re-layouts  2 us

profile of v1, /device:TPU:0, one launch (start us, length us, event | category | flops | bytes accessed | tf_op | source)
XLA Modules:
  0.0 67.9 jit_solution(2063676336982728372)
XLA Ops:
  0.6 65.2 %shard_map.68 = (bf16[4,1,32,128]{3,2,1,0:T(8,128)(2,1)}, bf16[4,1,32,128]{3,2,1,0:T(8,128)(2,1)}) custom-call(bf16[4,1,32,128]{3,2,1,0:T(8,128)(2,1)} %rhs_ref.1, s32[4,1,6]{2,1,0:T(1,128)} %pat_ref.1, bf16[4,1,6,128,128]{4,3,2,1,0:T(8,128)(2,1)} %fac_ref.1, bf16[4,1,128,128]{3,2,1,0:T(8,128)(2,1)} %inv_ref.1, s32[6]{0:T(128)} %size_ref.1), custom_call_target="tpu_custom_call" | custom-call | tf_op jit(solution)/shard_map/pallas_call | solution.py:371
  65.9 0.0 copy-start
  65.9 1.4 %copy.9 = bf16[4,1,32,128]{3,2,1,0:T(8,128)(2,1)} copy(bf16[4,1,32,128]{3,2,1,0:T(8,128)(2,1)} %get-tuple-element.4) | data formatting | bytes 65536
  67.3 0.0 copy-done
  67.3 0.6 copy.10
Async XLA Ops:
  65.9 1.4 %copy-start = (bf16[4,1,32,128]{3,2,1,0:T(8,128)(2,1)S(1)}, bf16[4,1,32,128]{3,2,1,0:T(8,128)(2,1)}, u32[]{:S(2)}) copy-start(bf16[4,1,32,128]{3,2,1,0:T(8,128)(2,1)} %get-tuple-element.5) | copy-start | bytes 98308

commit v2 on v1

--- a/solution.py
+++ b/solution.py
@@ -16,14 +16,17 @@
     n_chain,
     n_col,
     levels,
-    rhs_ref,
+    rhs_hbm,
     pat_ref,
     fac_ref,
-    inv_ref,
+    inv_hbm,
     size_ref,
     half_out,
     solved_out,
     fb,
+    rhs_ref,
+    inv_ref,
+    in_sem,
     pat_v,
     pat_s,
     code_s,
@@ -58,6 +61,12 @@
     so_send,
     so_recv,
 ):
+    loads = [
+        pltpu.make_async_copy(rhs_hbm, rhs_ref, in_sem.at[0]),
+        pltpu.make_async_copy(inv_hbm, inv_ref, in_sem.at[1]),
+    ]
+    for copy in loads:
+        copy.start()
     rows = rhs_ref.shape[0]
     probes = rhs_ref.shape[2]
     width = rhs_ref.shape[3]
@@ -169,6 +178,8 @@
         slot.append(here)
         live.append(count > 0)
 
+    for copy in loads:
+        copy.wait()
     for row in range(rows):
         rhs_f[row] = rhs_ref[row, 0].astype(F32)
 
@@ -367,20 +378,23 @@
     total = entries * n_col
     dma = pltpu.SemaphoreType.DMA
     vmem = pl.BlockSpec(memory_space=pltpu.VMEM)
-    out = jax.ShapeDtypeStruct(rhs.shape, rhs.dtype)
+    out = pltpu.VMEM(rhs.shape, rhs.dtype)
     return pl.pallas_call(
         functools.partial(kernel, n_chain, n_col, levels),
         out_shape=(out, out),
         in_specs=[
-            vmem,
-            vmem,
             pl.BlockSpec(memory_space=pl.ANY),
-            vmem,
+            pl.BlockSpec(memory_space=pl.ANY),
+            pl.BlockSpec(memory_space=pl.ANY),
+            pl.BlockSpec(memory_space=pl.ANY),
             pl.BlockSpec(memory_space=pltpu.SMEM),
         ],
         out_specs=(vmem, vmem),
         scratch_shapes=[
             pltpu.VMEM((rows, total, width, width), BF16),
+            pltpu.VMEM(rhs.shape, BF16),
+            pltpu.VMEM(inverse.shape, BF16),
+            dma((2,)),
             pltpu.VMEM((n_col, rows, 1, entries), jnp.int32),
             pltpu.SMEM((n_col, rows, 1, entries), jnp.int32),
             pltpu.SMEM((levels, total), jnp.int32),

time: 68.1 us -> 66.5 us (0.977)
  Pallas kernels: 65.2 us -> 64.4 us
  local copies, waits for them, and re-layouts: 2 us -> 1.23 us
    pallas_call x1, Pallas kernels: 65.2 us -> 64.4 us  [per_device(): pl.pallas_call(functools.partial(kernel, n_chain, n_col, levels), out_sha...]
    unnamed x4 -> x2, local copies, waits for them, and re-layouts: 2 us -> 1.23 us
where the time goes in v2:
time: 66.5 us; the launch traced here: 66.3 us
  Pallas kernels  64.4 us (97%)
  local copies, waits for them, and re-layouts  1.23 us (2%)
    pallas_call x1, Pallas kernels, per_device(): pl.pallas_call(functools.partial(kernel, n_chain, n_col, levels), out_sha...  64.4 us

profile of v2, /device:TPU:0, one launch (start us, length us, event | category | flops | bytes accessed | tf_op | source)
XLA Modules:
  0.0 66.3 jit_solution(10117020564032500907)
XLA Ops:
  0.6 64.4 %shard_map.68 = (bf16[4,1,32,128]{3,2,1,0:T(8,128)(2,1)S(1)}, bf16[4,1,32,128]{3,2,1,0:T(8,128)(2,1)S(1)}) custom-call(bf16[4,1,32,128]{3,2,1,0:T(8,128)(2,1)} %rhs_hbm.1, s32[4,1,6]{2,1,0:T(1,128)} %pat_ref.1, bf16[4,1,6,128,128]{4,3,2,1,0:T(8,128)(2,1)} %fac_ref.1, bf16[4,1,128,128]{3,2,1,0:T(8,128)(2,1)} %inv_hbm.1, s32[6]{0:T(128)} %size_ref.1), custom_call_target="tpu_custom_call" | custom-call | tf_op jit(solution)/shard_map/pallas_call | solution.py:382
  65.1 0.6 copy.9
  65.7 0.6 copy.10
